TPU v7x, 32 devices: a whole 2x2x4 slice. The times are simulated.
32 devices in a mesh: dz: 4 (over x, core), dxy: 8 (over z, y).
Axes of the slice: x: 2, y: 2, z: 4, core: 2. Of those that a mesh axis runs over, the one named last changes fastest.
Arguments:
- queries: bfloat16 [4096, 1024], P(('dz', 'dxy')), may hold values from -180 to 180
- keys: bfloat16 [4096, 1024], P(('dz', 'dxy')), may hold values from -4 to 4
- values: bfloat16 [4096, 1024], P(('dz', 'dxy')), may hold values from -6 to 6
- out_grad: bfloat16 [4096, 1024], P(('dz', 'dxy')), may hold values from -6 to 6
- out_weight: bfloat16 [1024, 1024], replicated, may hold values from -0.1875 to 0.1875
- pair_counts: int32 [32, 9], P(('dz', 'dxy')), may hold values from 0 to 128, as said below
- counts: int32 [32], P(('dz', 'dxy')), may hold values from 2 to 128
Outputs:
- gradient_of_queries: bfloat16 [4096, 1024], P(('dz', 'dxy'))
- gradient_of_keys: bfloat16 [4096, 1024], P(('dz', 'dxy'))
- gradient_of_values: bfloat16 [4096, 1024], P(('dz', 'dxy'))
- wo_grad: float32 [1024, 1024], P('dxy')
Inputs may be any that keep to these rules, and one draw needn't show every extreme that they name: `pair_counts`: slot ((i + 1) * 3 + (j + 1)) + t of cell c refers to cell t of the domain at offset (i, j) from c's domain; its entry is that cell's entry of counts when the two cells are linked, else 0, and always 0 where the domain lies outside the grid. Links are symmetric and every cell is linked to itself.
All inputs are finite; a program needn't handle non-finite values.
Results may differ from a plain program's by a relative error of at most 0.02.
Values may be sent and summed in bfloat16 or wider, within the bound.
No kernel may reach another device: no remote copies, remote signals or barrier semaphores. Data moves between devices by JAX's collectives and lax.ppermute only.
A program may use at most 128 MiB of HBM per device.

v0:
```python
import jax
import jax.numpy as jnp
from jax import lax
from jax.sharding import PartitionSpec as P

HEADS = 16
CELL = 128
GROUP_HEADS = 4


def extended(block, sides, width):
    for axis, dim in sides:
        count = lax.axis_size(axis)
        forward = [(i, i + 1) for i in range(count - 1)]
        backward = [(target, source) for source, target in forward]
        low = lax.ppermute(
            lax.slice_in_dim(block, block.shape[dim] - width, None, axis=dim), axis, forward
        )
        high = lax.ppermute(lax.slice_in_dim(block, 0, width, axis=dim), axis, backward)
        block = jnp.concatenate([low, block, high], axis=dim)
    return block


def shifted(value, axis, by):
    count = lax.axis_size(axis)
    pairs = [(i, i + by) for i in range(count) if 0 <= i + by < count]
    return lax.ppermute(value, axis, pairs)


def shards(queries, keys, values, out_grad, out_weight, pair_counts, counts):
    row_count, model_width = queries.shape
    head_width = model_width // HEADS
    logit_scale = head_width ** (-0.5)
    local_cells = counts.shape[0]
    key_rows = pair_counts.shape[1] * CELL
    group_width = GROUP_HEADS * head_width
    atom_index = jnp.arange(CELL, dtype=jnp.int32)
    live_rows = (atom_index[None, :] < counts[:, None]).reshape(row_count, 1)
    masked_grad = jnp.where(live_rows, out_grad, jnp.zeros_like(out_grad))
    out_delta = jnp.dot(masked_grad, out_weight, preferred_element_type=jnp.float32).astype(
        jnp.bfloat16
    )
    stacked = jnp.concatenate([keys, values], axis=1)[None, None]
    surround = extended(stacked, (("dz", 0), ("dxy", 1)), 1)
    surround = surround.reshape(key_rows, 2 * model_width)
    adjacent_keys = surround[:, :model_width]
    adjacent_values = surround[:, model_width:]
    allowed = (atom_index[None, None, :] < pair_counts[:, :, None]).reshape(local_cells, key_rows)
    allowed = jnp.repeat(allowed, CELL, axis=0)[None]
    query_parts, attended_parts, lse_parts, delta_parts, near_key_parts, near_value_parts = (
        [],
        [],
        [],
        [],
        [],
        [],
    )
    for group_id in range(HEADS // GROUP_HEADS):
        columns = slice(group_id * group_width, (group_id + 1) * group_width)
        cluster_queries = queries[:, columns].reshape(row_count, GROUP_HEADS, head_width)
        cluster_delta = out_delta[:, columns].reshape(row_count, GROUP_HEADS, head_width)
        cluster_keys = adjacent_keys[:, columns].reshape(key_rows, GROUP_HEADS, head_width)
        cluster_values = adjacent_values[:, columns].reshape(key_rows, GROUP_HEADS, head_width)
        attention_logits = logit_scale * jnp.einsum(
            "qvy,pvy->vqp", cluster_queries, cluster_keys, preferred_element_type=jnp.float32
        )
        attention_logits = jnp.where(allowed, attention_logits, -1e30)
        highest = jnp.max(attention_logits, axis=-1, keepdims=True)
        weight_sum = jnp.sum(
            jnp.where(allowed, jnp.exp(attention_logits - highest), 0.0), axis=-1, keepdims=True
        )
        log_total = highest + jnp.log(weight_sum)
        probs = jnp.where(allowed, jnp.exp(attention_logits - log_total), 0.0)
        probabilities_reduced = probs.astype(jnp.bfloat16)
        attention_result = jnp.einsum(
            "gtl,lgs->tgs",
            probabilities_reduced,
            cluster_values,
            preferred_element_type=jnp.float32,
        ).astype(jnp.bfloat16)
        row_delta = jnp.sum(
            cluster_delta.astype(jnp.float32) * attention_result.astype(jnp.float32), axis=-1
        )
        probability_gradient = jnp.einsum(
            "qvy,pvy->vqp", cluster_delta, cluster_values, preferred_element_type=jnp.float32
        )
        score_gradient = (probs * (probability_gradient - row_delta.T[:, :, None])).astype(
            jnp.bfloat16
        )
        group_grad = logit_scale * jnp.einsum(
            "gtl,lgs->tgs", score_gradient, cluster_keys, preferred_element_type=jnp.float32
        )
        query_parts.append(group_grad.astype(jnp.bfloat16).reshape(row_count, group_width))
        attended_parts.append(attention_result.reshape(row_count, group_width))
        lse_parts.append(log_total[:, :, 0])
        delta_parts.append(row_delta.T)
        value_part = jnp.einsum(
            "snq,nst->qst", probabilities_reduced, cluster_delta, preferred_element_type=jnp.float32
        )
        key_part = logit_scale * jnp.einsum(
            "snq,nst->qst", score_gradient, cluster_queries, preferred_element_type=jnp.float32
        )
        near_key_parts.append(key_part.reshape(key_rows, group_width))
        near_value_parts.append(value_part.reshape(key_rows, group_width))
    gradient_of_queries = jnp.concatenate(query_parts, axis=1)
    attended_all = jnp.concatenate(attended_parts, axis=1)
    key_partials = jnp.concatenate(near_key_parts + near_value_parts, axis=1).reshape(
        3, 3, row_count, 2 * model_width
    )
    column_sums = key_partials[1]
    for layer_slot, offset in ((0, -1), (2, 1)):
        column_sums = column_sums + shifted(key_partials[layer_slot], "dz", offset)
    owned = column_sums[1]
    for place_slot, offset in ((0, -1), (2, 1)):
        owned = owned + shifted(column_sums[place_slot], "dxy", offset)
    gradient_of_keys = owned[:, :model_width].astype(jnp.bfloat16)
    gradient_of_values = owned[:, model_width:].astype(jnp.bfloat16)
    device_count = lax.axis_size("dz") * lax.axis_size("dxy")
    normalizer = (row_count * device_count) ** (-0.5)
    plane_rows = lax.psum_scatter(
        lax.dot_general(
            masked_grad, attended_all, (((0,), (0,)), ((), ())), preferred_element_type=jnp.float32
        ),
        "dxy",
        scatter_dimension=0,
        tiled=True,
    )
    wo_grad = lax.psum(plane_rows, "dz") * normalizer
    return (gradient_of_queries, gradient_of_keys, gradient_of_values, wo_grad)


def solution(mesh):
    in_specs = (
        P(("dz", "dxy"), None),
        P(("dz", "dxy"), None),
        P(("dz", "dxy"), None),
        P(("dz", "dxy"), None),
        P(),
        P(("dz", "dxy"), None),
        P(("dz", "dxy")),
    )
    out_specs = (
        P(("dz", "dxy"), None),
        P(("dz", "dxy"), None),
        P(("dz", "dxy"), None),
        P("dxy", None),
    )
    return jax.shard_map(shards, mesh=mesh, in_specs=in_specs, out_specs=out_specs, check_vma=False)
```

profile of v0, /device:TPU:0, one launch (start us, length us, event | category | flops | bytes accessed | tf_op | source)
XLA Modules:
  0.0 288.1 jit_solution(11194550064958345261)
XLA Ops:
  9.8 3.1 %collective-permute-start = (bf16[1,1,128,2048]{3,2,1,0:T(8,128)(2,1)S(1)}, bf16[1,1,128,2048]{3,2,1,0:T(8,128)(2,1)S(1)}, u32[]{:S(2)}, u32[]{:S(2)}) collective-permute-start(bf16[1,1,128,2048]{3,2,1,0:T(8,128)(2,1)S(1)} %maximum_bitcast_fusion), channel_id=1, source_target_pairs={{0,8},{8,16},{16,24},{1,9},{9,17},{17,25},{2,10},{10,18},{18,26},{... | collective-permute-start | bytes 1572872 | tf_op jit(solution)/shard_map/ppermute | solution.py:16
  17.0 6.7 %collective-permute-start.2 = (bf16[3,1,128,2048]{3,2,1,0:T(8,128)(2,1)}, bf16[3,1,128,2048]{3,2,1,0:T(8,128)(2,1)}, u32[]{:S(2)}, u32[]{:S(2)}) collective-permute-start(bf16[3,1,128,2048]{3,2,1,0:T(8,128)(2,1)} %pad_maximum_fusion.1), channel_id=1, source_target_pairs={{0,1},{1,2},{2,3},{3,4},{4,5},{5,6},{6,7},{8,9},{9,10},{10,11},{11... | collective-permute-start | bytes 4718600 | tf_op jit(solution)/shard_map/ppermute | solution.py:16
  31.8 19.1 %collective-permute-done.3 = bf16[3,1,128,2048]{3,2,1,0:T(8,128)(2,1)} collective-permute-done((bf16[3,1,128,2048]{3,2,1,0:T(8,128)(2,1)}, bf16[3,1,128,2048]{3,2,1,0:T(8,128)(2,1)}, u32[]{:S(2)}, u32[]{:S(2)}) %collective-permute-start.3) | collective-permute-done | bytes 1572896 | tf_op jit(solution)/shard_map/ppermute | solution.py:19
  50.9 39.3 %collective-permute-done.2 = bf16[3,1,128,2048]{3,2,1,0:T(8,128)(2,1)} collective-permute-done((bf16[3,1,128,2048]{3,2,1,0:T(8,128)(2,1)}, bf16[3,1,128,2048]{3,2,1,0:T(8,128)(2,1)}, u32[]{:S(2)}, u32[]{:S(2)}) %collective-permute-start.2) | collective-permute-done | bytes 1572896 | tf_op jit(solution)/shard_map/ppermute | solution.py:16
  90.2 2.3 pad_maximum_fusion
  102.0 1.6 fusion.56
  106.0 2.3 select_reduce_fusion.3
  108.9 1.7 fusion.47
  123.2 2.8 fusion.27
  133.6 3.3 %fusion.50 = (f32[384,2048]{0,1:T(8,128)}, f32[384,2048]{0,1:T(8,128)}, f32[384,2048]{0,1:T(8,128)S(1)}) fusion(f32[1152,2048]{0,1:T(8,128)S(1)} %constant_dynamic-update-slice_fusion), kind=kLoop, calls=%fused_computation.100 | loop fusion | bytes 18874368 | tf_op jit(solution)/shard_map/slice | solution.py:112
  137.0 3.5 %copy.103 = f32[384,2048]{1,0:T(8,128)} copy(f32[384,2048]{0,1:T(8,128)} %get-tuple-element.8) | data formatting | bytes 6291456 | tf_op jit(solution)/shard_map/slice | solution.py:112
  140.5 3.6 %copy.104 = f32[384,2048]{1,0:T(8,128)} copy(f32[384,2048]{0,1:T(8,128)} %get-tuple-element.9) | data formatting | bytes 6291456 | tf_op jit(solution)/shard_map/slice | solution.py:112
  144.1 3.9 %collective-permute-start.5 = (f32[3,128,2048]{2,1,0:T(8,128)}, f32[3,128,2048]{2,1,0:T(8,128)}, u32[]{:S(2)}, u32[]{:S(2)}) collective-permute-start(f32[3,128,2048]{2,1,0:T(8,128)} %bitcast.169), channel_id=1, source_target_pairs={{0,8},{8,16},{16,24},{1,9},{9,17},{17,25},{2,10},{10,18},{18,26},{... | collective-permute-start | bytes 9437192 | tf_op jit(solution)/shard_map/ppermute | solution.py:27
  149.3 2.3 copy.102
  151.9 4.0 %collective-permute-done.4 = f32[3,128,2048]{2,1,0:T(8,128)} collective-permute-done((f32[3,128,2048]{2,1,0:T(8,128)}, f32[3,128,2048]{2,1,0:T(8,128)}, u32[]{:S(2)}, u32[]{:S(2)}) %collective-permute-start.4) | collective-permute-done | bytes 3145760 | tf_op jit(solution)/shard_map/ppermute | solution.py:27
  155.9 4.7 %add_add_fusion = f32[3,128,2048]{2,1,0:T(8,128)S(1)} fusion(f32[3,128,2048]{2,1,0:T(8,128)} %collective-permute-done.5, f32[3,128,2048]{2,1,0:T(8,128)} %bitcast.151, f32[3,128,2048]{2,1,0:T(8,128)} %collective-permute-done.4), kind=kLoop, calls=%fused_computation.21 | loop fusion | flops 1572864 | bytes 12582912 | tf_op jit(solution)/shard_map/add | solution.py:112
  160.7 1.7 copy-done.6
  165.2 5.9 %collective-permute-start.7 = (f32[128,2048]{1,0:T(8,128)}, f32[128,2048]{1,0:T(8,128)}, u32[]{:S(2)}, u32[]{:S(2)}) collective-permute-start(f32[128,2048]{1,0:T(8,128)} %get-tuple-element.20), channel_id=1, source_target_pairs={{0,1},{1,2},{2,3},{3,4},{4,5},{5,6},{6,7},{8,9},{9,10},{10,11},{11... | collective-permute-start | bytes 3145736 | tf_op jit(solution)/shard_map/ppermute | solution.py:27
  172.1 1.7 copy.90
  173.8 2.1 fusion.21
  180.7 63.3 %reduce-scatter.2.cloned.1.call-done = f32[128,1024]{1,0:T(8,128)} async-done(((f32[1024,1024]{1,0:T(8,128)}), f32[128,1024]{1,0:T(8,128)}) %reduce-scatter.2.cloned.1.call-update) | async-done | bytes 524304 | tf_op jit(solution)/shard_map/reduce_scatter | solution.py:120
  244.0 2.2 fusion.26
  247.0 32.3 %all-reduce.2.cloned.1.call-done = f32[128,1024]{1,0:T(8,128)} async-done(((f32[128,1024]{1,0:T(8,128)}), f32[128,1024]{1,0:T(8,128)}) %all-reduce.2.cloned.1.call-update) | async-done | bytes 524304 | tf_op jit(solution)/shard_map/psum | solution.py:128
  279.4 1.9 broadcast_multiply_fusion
  (164 shorter events, 57.5 us)
Async XLA Ops:
  7.2 17.2 %copy-start = (bf16[1024,1024]{1,0:T(8,128)(2,1)S(1)}, bf16[1024,1024]{1,0:T(8,128)(2,1)}, u32[]{:S(2)}) copy-start(bf16[1024,1024]{1,0:T(8,128)(2,1)} %param.11) | copy-start | bytes 6291460
  7.2 17.2 %copy-start.28 = (bf16[128,1024]{1,0:T(8,128)(2,1)S(1)}, bf16[128,1024]{1,0:T(8,128)(2,1)}, u32[]{:S(2)}) copy-start(bf16[128,1024]{1,0:T(8,128)(2,1)} %param.10) | copy-start | bytes 786436
  7.2 236.8 %reduce-scatter.2.cloned.1.call-start = ((), (), s32[]{:S(2)}) async-start(), calls=%async_computation.1 | async-start | bytes 4718592 | tf_op jit(solution)/shard_map/reduce_scatter | solution.py:120
  8.5 4.4 %collective-permute-start.1 = (bf16[1,1,128,2048]{3,2,1,0:T(8,128)(2,1)S(1)}, bf16[1,1,128,2048]{3,2,1,0:T(8,128)(2,1)S(1)}, u32[]{:S(2)}, u32[]{:S(2)}) collective-permute-start(bf16[1,1,128,2048]{3,2,1,0:T(8,128)(2,1)S(1)} %maximum_bitcast_fusion), channel_id=1, source_target_pairs={{8,0},{16,8},{24,16},{9,1},{17,9},{25,17},{10,2},{18,10},{26,18},{... | collective-permute-start | bytes 1572872 | tf_op jit(solution)/shard_map/ppermute | solution.py:19
  9.8 4.6 %collective-permute-start = (bf16[1,1,128,2048]{3,2,1,0:T(8,128)(2,1)S(1)}, bf16[1,1,128,2048]{3,2,1,0:T(8,128)(2,1)S(1)}, u32[]{:S(2)}, u32[]{:S(2)}) collective-permute-start(bf16[1,1,128,2048]{3,2,1,0:T(8,128)(2,1)S(1)} %maximum_bitcast_fusion), channel_id=1, source_target_pairs={{0,8},{8,16},{16,24},{1,9},{9,17},{17,25},{2,10},{10,18},{18,26},{... | collective-permute-start | bytes 1572872 | tf_op jit(solution)/shard_map/ppermute | solution.py:16
  14.3 10.6 %copy-start.27 = (bf16[1,1,128,2048]{3,2,1,0:T(8,128)(2,1)}, bf16[1,1,128,2048]{3,2,1,0:T(8,128)(2,1)S(1)}, u32[]{:S(2)}) copy-start(bf16[1,1,128,2048]{3,2,1,0:T(8,128)(2,1)S(1)} %collective-permute-done) | copy-start | bytes 1572868
  15.7 35.2 %collective-permute-start.3 = (bf16[3,1,128,2048]{3,2,1,0:T(8,128)(2,1)}, bf16[3,1,128,2048]{3,2,1,0:T(8,128)(2,1)}, u32[]{:S(2)}, u32[]{:S(2)}) collective-permute-start(bf16[3,1,128,2048]{3,2,1,0:T(8,128)(2,1)} %pad_maximum_fusion.1), channel_id=1, source_target_pairs={{1,0},{2,1},{3,2},{4,3},{5,4},{6,5},{7,6},{9,8},{10,9},{11,10},{12... | collective-permute-start | bytes 4718600 | tf_op jit(solution)/shard_map/ppermute | solution.py:19
  17.0 73.2 %collective-permute-start.2 = (bf16[3,1,128,2048]{3,2,1,0:T(8,128)(2,1)}, bf16[3,1,128,2048]{3,2,1,0:T(8,128)(2,1)}, u32[]{:S(2)}, u32[]{:S(2)}) collective-permute-start(bf16[3,1,128,2048]{3,2,1,0:T(8,128)(2,1)} %pad_maximum_fusion.1), channel_id=1, source_target_pairs={{0,1},{1,2},{2,3},{3,4},{4,5},{5,6},{6,7},{8,9},{9,10},{10,11},{11... | collective-permute-start | bytes 4718600 | tf_op jit(solution)/shard_map/ppermute | solution.py:16
  24.4 7.3 %copy-start.44 = (s32[1,9]{1,0:T(1,128)S(1)}, s32[1,9]{1,0:T(1,128)}, u32[]{:S(2)}) copy-start(s32[1,9]{1,0:T(1,128)} %param.12) | copy-start | bytes 112
  95.5 9.7 %copy-start.15 = (bf16[1152,256]{0,1:T(8,128)(2,1)}, bf16[1152,256]{0,1:T(8,128)(2,1)S(1)}, u32[]{:S(2)}) copy-start(bf16[1152,256]{0,1:T(8,128)(2,1)S(1)} %copy.131) | copy-start | bytes 1769476
  97.9 6.4 %copy-start.16 = (bf16[1152,256]{0,1:T(8,128)(2,1)}, bf16[1152,256]{0,1:T(8,128)(2,1)S(1)}, u32[]{:S(2)}) copy-start(bf16[1152,256]{0,1:T(8,128)(2,1)S(1)} %copy.129) | copy-start | bytes 1769476
  104.4 8.5 %copy-start.4 = (f32[4,128,1152]{1,2,0:T(8,128)}, f32[4,128,1152]{1,2,0:T(8,128)S(1)}, u32[]{:S(2)}) copy-start(f32[4,128,1152]{1,2,0:T(8,128)S(1)} %get-tuple-element.36) | copy-start | bytes 7077892
  105.2 11.0 %copy-start.2 = (f32[4,128,1152]{1,2,0:T(8,128)}, f32[4,128,1152]{1,2,0:T(8,128)S(1)}, u32[]{:S(2)}) copy-start(f32[4,128,1152]{1,2,0:T(8,128)S(1)} %get-tuple-element.38) | copy-start | bytes 7077892
  126.0 153.4 %all-reduce.2.cloned.1.call-start = ((), (), s32[]{:S(2)}) async-start(), calls=%async_computation.2 | async-start | bytes 1048576 | tf_op jit(solution)/shard_map/psum | solution.py:128
  144.1 7.8 %collective-permute-start.5 = (f32[3,128,2048]{2,1,0:T(8,128)}, f32[3,128,2048]{2,1,0:T(8,128)}, u32[]{:S(2)}, u32[]{:S(2)}) collective-permute-start(f32[3,128,2048]{2,1,0:T(8,128)} %bitcast.169), channel_id=1, source_target_pairs={{0,8},{8,16},{16,24},{1,9},{9,17},{17,25},{2,10},{10,18},{18,26},{... | collective-permute-start | bytes 9437192 | tf_op jit(solution)/shard_map/ppermute | solution.py:27
  148.0 7.9 %collective-permute-start.4 = (f32[3,128,2048]{2,1,0:T(8,128)}, f32[3,128,2048]{2,1,0:T(8,128)}, u32[]{:S(2)}, u32[]{:S(2)}) collective-permute-start(f32[3,128,2048]{2,1,0:T(8,128)} %bitcast.168), channel_id=1, source_target_pairs={{8,0},{16,8},{24,16},{9,1},{17,9},{25,17},{10,2},{18,10},{26,18},{... | collective-permute-start | bytes 9437192 | tf_op jit(solution)/shard_map/ppermute | solution.py:27
  162.3 8.8 %copy-start.8 = (bf16[4,128,1152]{1,2,0:T(8,128)(2,1)S(1)}, bf16[4,128,1152]{1,2,0:T(8,128)(2,1)}, u32[]{:S(2)}) copy-start(bf16[4,128,1152]{1,2,0:T(8,128)(2,1)} %copy-done.7) | copy-start | bytes 3538948
  162.3 8.8 %copy-start.19 = (bf16[1152,256]{0,1:T(8,128)(2,1)S(1)}, bf16[1152,256]{0,1:T(8,128)(2,1)}, u32[]{:S(2)}) copy-start(bf16[1152,256]{0,1:T(8,128)(2,1)} %copy-done.18) | copy-start | bytes 1769476
  162.3 11.5 %copy-start.10 = (bf16[4,128,1152]{1,2,0:T(8,128)(2,1)S(1)}, bf16[4,128,1152]{1,2,0:T(8,128)(2,1)}, u32[]{:S(2)}) copy-start(bf16[4,128,1152]{1,2,0:T(8,128)(2,1)} %copy-done.9) | copy-start | bytes 3538948
  163.8 13.1 %copy-start.12 = (bf16[4,128,1152]{1,2,0:T(8,128)(2,1)S(1)}, bf16[4,128,1152]{1,2,0:T(8,128)(2,1)}, u32[]{:S(2)}) copy-start(bf16[4,128,1152]{1,2,0:T(8,128)(2,1)} %copy-done.11) | copy-start | bytes 3538948
  163.8 80.2 %collective-permute-start.6 = (f32[128,2048]{1,0:T(8,128)}, f32[128,2048]{1,0:T(8,128)}, u32[]{:S(2)}, u32[]{:S(2)}) collective-permute-start(f32[128,2048]{1,0:T(8,128)} %get-tuple-element.19), channel_id=1, source_target_pairs={{1,0},{2,1},{3,2},{4,3},{5,4},{6,5},{7,6},{9,8},{10,9},{11,10},{12... | collective-permute-start | bytes 3145736 | tf_op jit(solution)/shard_map/ppermute | solution.py:27
  165.2 78.8 %collective-permute-start.7 = (f32[128,2048]{1,0:T(8,128)}, f32[128,2048]{1,0:T(8,128)}, u32[]{:S(2)}, u32[]{:S(2)}) collective-permute-start(f32[128,2048]{1,0:T(8,128)} %get-tuple-element.20), channel_id=1, source_target_pairs={{0,1},{1,2},{2,3},{3,4},{4,5},{5,6},{6,7},{8,9},{9,10},{10,11},{11... | collective-permute-start | bytes 3145736 | tf_op jit(solution)/shard_map/ppermute | solution.py:27
  172.1 6.3 %copy-start.14 = (bf16[4,128,1152]{1,2,0:T(8,128)(2,1)S(1)}, bf16[4,128,1152]{1,2,0:T(8,128)(2,1)}, u32[]{:S(2)}) copy-start(bf16[4,128,1152]{1,2,0:T(8,128)(2,1)} %copy-done.13) | copy-start | bytes 3538948
  244.0 37.2 %copy-start.1 = (bf16[1024,1024]{1,0:T(8,128)(2,1)S(1)}, bf16[1024,1024]{1,0:T(8,128)(2,1)}, u32[]{:S(2)}) copy-start(bf16[1024,1024]{1,0:T(8,128)(2,1)} %param.11) | copy-start | bytes 6291460
  (31 other events, 64.3 us)
Sparse Core Ops, SparseCore 0:
  126.1 117.8 reduce-scatter.1
  246.3 32.9 all-reduce.1
where the time goes:
time: 289 us; the launch traced here: 288 us
  waiting for transfers between devices  160 us (55%)
  local copies, waits for them, and re-layouts  42.7 us (15%)
  matrix products  28.6 us (10%)
  starting transfers between devices  25 us (9%)
  other arithmetic  16.7 us (6%)
  between operations  15.4 us (5%)
    reduce_scatter x1, waiting for transfers between devices, shards(): lax.psum_scatter(lax.dot_general(masked_grad, attended_all, (((0,), (0,))...  63.3 us
    ppermute x2, waiting for transfers between devices, extended(): lax.ppermute(lax.slice_in_dim(block, block.shape[dim] - width, None, axis...  40.7 us
    psum x1, waiting for transfers between devices, shards(): wo_grad = lax.psum(plane_rows, 'dz') * normalizer  32.3 us
    ppermute x2, waiting for transfers between devices, extended(): lax.ppermute(lax.slice_in_dim(block, 0, width, axis=dim), axis, backward)  19.1 us
    unnamed x105, local copies, waits for them, and re-layouts  16.4 us
    ppermute x4, starting transfers between devices, shifted(): return lax.ppermute(value, axis, pairs)  12.5 us
    slice x3, local copies, waits for them, and re-layouts, shards(): column_sums = column_sums + shifted(key_partials[layer_slot], 'dz', offset)  10.5 us
    ppermute x2, starting transfers between devices, extended(): lax.ppermute(lax.slice_in_dim(block, block.shape[dim] - width, None, axis...  9.78 us
  transfers between devices with their start and end apart: 10, of which 7 were waited for; matrix products, arithmetic and copies ran while one was open for 14% of the time, Pallas kernels for 0%

commit v1 on v0

--- a/solution.py
+++ b/solution.py
@@ -125,7 +125,7 @@
         scatter_dimension=0,
         tiled=True,
     )
-    wo_grad = lax.psum(plane_rows, "dz") * normalizer
+    wo_grad = jnp.sum(lax.all_gather(plane_rows, "dz"), axis=0) * normalizer
     return (gradient_of_queries, gradient_of_keys, gradient_of_values, wo_grad)
 
 

time: 289 us -> 279 us (0.965)
  waiting for transfers between devices: 160 us -> 152 us
    psum x1 -> x0, waiting for transfers between devices: 32.3 us -> none  [shards(): wo_grad = lax.psum(plane_rows, 'dz') * normalizer]
    ppermute x4, waiting for transfers between devices: 4.26 us -> 32.6 us  [shifted(): return lax.ppermute(value, axis, pairs)]
    reduce_scatter x1, waiting for transfers between devices: 63.3 us -> 59.6 us  [shards(): lax.psum_scatter(lax.dot_general(masked_grad, attended_all, (((0,), (0,))...]
    unnamed x105 -> x121, local copies, waits for them, and re-layouts: 16.4 us -> 15.6 us
  transfers between devices with their start and end apart: 10 -> 10, of which waited for: 7 -> 6; matrix products, arithmetic and copies ran while one was open for 14% -> 16% of each run, Pallas kernels for 0% -> 0%
where the time goes in v1:
time: 279 us; the launch traced here: 278 us
  waiting for transfers between devices  152 us (54%)
  local copies, waits for them, and re-layouts  41.9 us (15%)
  matrix products  26.6 us (10%)
  starting transfers between devices  24.6 us (9%)
  other arithmetic  17.4 us (6%)
  between operations  15.5 us (6%)
    reduce_scatter x1, waiting for transfers between devices, shards(): lax.psum_scatter(lax.dot_general(masked_grad, attended_all, (((0,), (0,))...  59.6 us
    ppermute x2, waiting for transfers between devices, extended(): lax.ppermute(lax.slice_in_dim(block, block.shape[dim] - width, None, axis...  40.7 us
    ppermute x4, waiting for transfers between devices, shifted(): return lax.ppermute(value, axis, pairs)  32.6 us
    ppermute x2, waiting for transfers between devices, extended(): lax.ppermute(lax.slice_in_dim(block, 0, width, axis=dim), axis, backward)  19.1 us
    unnamed x121, local copies, waits for them, and re-layouts  15.6 us
    ppermute x4, starting transfers between devices, shifted(): return lax.ppermute(value, axis, pairs)  12.2 us
    slice x3, local copies, waits for them, and re-layouts, shards(): column_sums = column_sums + shifted(key_partials[layer_slot], 'dz', offset)  10.4 us
    ppermute x2, starting transfers between devices, extended(): lax.ppermute(lax.slice_in_dim(block, block.shape[dim] - width, None, axis...  9.77 us
  transfers between devices with their start and end apart: 10, of which 6 were waited for; matrix products, arithmetic and copies ran while one was open for 16% of the time, Pallas kernels for 0%

profile of v1, /device:TPU:0, one launch (start us, length us, event | category | flops | bytes accessed | tf_op | source)
XLA Modules:
  0.0 278.1 jit_solution(3389136567641179599)
XLA Ops:
  9.8 3.1 %collective-permute-start = (bf16[1,1,128,2048]{3,2,1,0:T(8,128)(2,1)S(1)}, bf16[1,1,128,2048]{3,2,1,0:T(8,128)(2,1)S(1)}, u32[]{:S(2)}, u32[]{:S(2)}) collective-permute-start(bf16[1,1,128,2048]{3,2,1,0:T(8,128)(2,1)S(1)} %maximum_bitcast_fusion), channel_id=1, source_target_pairs={{0,8},{8,16},{16,24},{1,9},{9,17},{17,25},{2,10},{10,18},{18,26},{... | collective-permute-start | bytes 1572872 | tf_op jit(solution)/shard_map/ppermute | solution.py:16
  17.0 6.7 %collective-permute-start.2 = (bf16[3,1,128,2048]{3,2,1,0:T(8,128)(2,1)}, bf16[3,1,128,2048]{3,2,1,0:T(8,128)(2,1)}, u32[]{:S(2)}, u32[]{:S(2)}) collective-permute-start(bf16[3,1,128,2048]{3,2,1,0:T(8,128)(2,1)} %pad_maximum_fusion.1), channel_id=1, source_target_pairs={{0,1},{1,2},{2,3},{3,4},{4,5},{5,6},{6,7},{8,9},{9,10},{10,11},{11... | collective-permute-start | bytes 4718600 | tf_op jit(solution)/shard_map/ppermute | solution.py:16
  31.8 19.1 %collective-permute-done.3 = bf16[3,1,128,2048]{3,2,1,0:T(8,128)(2,1)} collective-permute-done((bf16[3,1,128,2048]{3,2,1,0:T(8,128)(2,1)}, bf16[3,1,128,2048]{3,2,1,0:T(8,128)(2,1)}, u32[]{:S(2)}, u32[]{:S(2)}) %collective-permute-start.3) | collective-permute-done | bytes 1572896 | tf_op jit(solution)/shard_map/ppermute | solution.py:19
  50.9 39.3 %collective-permute-done.2 = bf16[3,1,128,2048]{3,2,1,0:T(8,128)(2,1)} collective-permute-done((bf16[3,1,128,2048]{3,2,1,0:T(8,128)(2,1)}, bf16[3,1,128,2048]{3,2,1,0:T(8,128)(2,1)}, u32[]{:S(2)}, u32[]{:S(2)}) %collective-permute-start.2) | collective-permute-done | bytes 1572896 | tf_op jit(solution)/shard_map/ppermute | solution.py:16
  90.2 2.3 pad_maximum_fusion
  99.3 1.6 copy.125
  101.9 1.6 fusion.56
  105.9 2.3 select_reduce_fusion.3
  116.4 2.8 %fusion.27 = f32[1024,1024]{1,0:T(8,128)} fusion(bf16[128,256]{0,1:T(8,128)(2,1)S(1)} %bitcast.202, bf16[128,256]{0,1:T(8,128)(2,1)S(1)} %bitcast.203, bf16[128,256]{0,1:T(8,128)(2,1)S(1)} %bitcast.201, bf16[128,256]{0,1:T(8,128)(2,1)S(1)} %bitcast.200, bf16[128,1024]{1,0:T(8,128)(2,1)S(1)} %copy-done.30, pred[128]{0:T(512)(128)(4,1)S(1)} %copy-done.51), kind=kOutput, calls=%fused_computation.64 | convolution fusion | flops 269615104 | bytes 4718720 | tf_op jit(solution)/shard_map/dot_general | solution.py:121
  130.9 3.3 %fusion.50 = (f32[384,2048]{0,1:T(8,128)}, f32[384,2048]{0,1:T(8,128)}, f32[384,2048]{0,1:T(8,128)S(1)}) fusion(f32[1152,2048]{0,1:T(8,128)S(1)} %constant_dynamic-update-slice_fusion), kind=kLoop, calls=%fused_computation.100 | loop fusion | bytes 18874368 | tf_op jit(solution)/shard_map/slice | solution.py:112
  134.2 3.6 %copy.103 = f32[384,2048]{1,0:T(8,128)} copy(f32[384,2048]{0,1:T(8,128)} %get-tuple-element.8) | data formatting | bytes 6291456 | tf_op jit(solution)/shard_map/slice | solution.py:112
  137.7 3.6 %copy.104 = f32[384,2048]{1,0:T(8,128)} copy(f32[384,2048]{0,1:T(8,128)} %get-tuple-element.9) | data formatting | bytes 6291456 | tf_op jit(solution)/shard_map/slice | solution.py:112
  141.3 3.8 %collective-permute-start.5 = (f32[3,128,2048]{2,1,0:T(8,128)}, f32[3,128,2048]{2,1,0:T(8,128)}, u32[]{:S(2)}, u32[]{:S(2)}) collective-permute-start(f32[3,128,2048]{2,1,0:T(8,128)} %bitcast.170), channel_id=1, source_target_pairs={{0,8},{8,16},{16,24},{1,9},{9,17},{17,25},{2,10},{10,18},{18,26},{... | collective-permute-start | bytes 9437192 | tf_op jit(solution)/shard_map/ppermute | solution.py:27
  146.4 2.4 copy.102
  148.8 59.6 %reduce-scatter.2.cloned.1.call-done = f32[128,1024]{1,0:T(8,128)} async-done(((f32[1024,1024]{1,0:T(8,128)}), f32[128,1024]{1,0:T(8,128)}) %reduce-scatter.2.cloned.1.call-update) | async-done | bytes 524304 | tf_op jit(solution)/shard_map/reduce_scatter | solution.py:120
  208.4 4.7 %add_add_fusion = f32[3,128,2048]{2,1,0:T(8,128)S(1)} fusion(f32[3,128,2048]{2,1,0:T(8,128)} %collective-permute-done.5, f32[3,128,2048]{2,1,0:T(8,128)} %bitcast.152, f32[3,128,2048]{2,1,0:T(8,128)} %collective-permute-done.4), kind=kLoop, calls=%fused_computation.21 | loop fusion | flops 1572864 | bytes 12582912 | tf_op jit(solution)/shard_map/add | solution.py:112
  213.1 1.7 copy-done.8
  217.9 5.5 %collective-permute-start.7 = (f32[128,2048]{1,0:T(8,128)}, f32[128,2048]{1,0:T(8,128)}, u32[]{:S(2)}, u32[]{:S(2)}) collective-permute-start(f32[128,2048]{1,0:T(8,128)} %get-tuple-element.20), channel_id=1, source_target_pairs={{0,1},{1,2},{2,3},{3,4},{4,5},{5,6},{6,7},{8,9},{9,10},{10,11},{11... | collective-permute-start | bytes 3145736 | tf_op jit(solution)/shard_map/ppermute | solution.py:27
  224.4 1.7 copy.90
  226.1 2.1 fusion.21
  233.0 10.2 %collective-permute-done.6 = f32[128,2048]{1,0:T(8,128)} collective-permute-done((f32[128,2048]{1,0:T(8,128)}, f32[128,2048]{1,0:T(8,128)}, u32[]{:S(2)}, u32[]{:S(2)}) %collective-permute-start.6) | collective-permute-done | bytes 1048608 | tf_op jit(solution)/shard_map/ppermute | solution.py:27
  243.2 22.4 %collective-permute-done.7 = f32[128,2048]{1,0:T(8,128)} collective-permute-done((f32[128,2048]{1,0:T(8,128)}, f32[128,2048]{1,0:T(8,128)}, u32[]{:S(2)}, u32[]{:S(2)}) %collective-permute-start.7) | collective-permute-done | bytes 1048608 | tf_op jit(solution)/shard_map/ppermute | solution.py:27
  265.6 2.2 fusion.26
  268.6 1.8 reduce_sum.89
  (181 shorter events, 55.4 us)
Async XLA Ops:
  7.2 17.2 %copy-start = (bf16[1024,1024]{1,0:T(8,128)(2,1)S(1)}, bf16[1024,1024]{1,0:T(8,128)(2,1)}, u32[]{:S(2)}) copy-start(bf16[1024,1024]{1,0:T(8,128)(2,1)} %param.11) | copy-start | bytes 6291460
  7.2 17.2 %copy-start.29 = (bf16[128,1024]{1,0:T(8,128)(2,1)S(1)}, bf16[128,1024]{1,0:T(8,128)(2,1)}, u32[]{:S(2)}) copy-start(bf16[128,1024]{1,0:T(8,128)(2,1)} %param.10) | copy-start | bytes 786436
  7.2 201.2 %reduce-scatter.2.cloned.1.call-start = ((), (), s32[]{:S(2)}) async-start(), calls=%async_computation.1 | async-start | bytes 4718592 | tf_op jit(solution)/shard_map/reduce_scatter | solution.py:120
  8.5 4.4 %collective-permute-start.1 = (bf16[1,1,128,2048]{3,2,1,0:T(8,128)(2,1)S(1)}, bf16[1,1,128,2048]{3,2,1,0:T(8,128)(2,1)S(1)}, u32[]{:S(2)}, u32[]{:S(2)}) collective-permute-start(bf16[1,1,128,2048]{3,2,1,0:T(8,128)(2,1)S(1)} %maximum_bitcast_fusion), channel_id=1, source_target_pairs={{8,0},{16,8},{24,16},{9,1},{17,9},{25,17},{10,2},{18,10},{26,18},{... | collective-permute-start | bytes 1572872 | tf_op jit(solution)/shard_map/ppermute | solution.py:19
  9.8 4.6 %collective-permute-start = (bf16[1,1,128,2048]{3,2,1,0:T(8,128)(2,1)S(1)}, bf16[1,1,128,2048]{3,2,1,0:T(8,128)(2,1)S(1)}, u32[]{:S(2)}, u32[]{:S(2)}) collective-permute-start(bf16[1,1,128,2048]{3,2,1,0:T(8,128)(2,1)S(1)} %maximum_bitcast_fusion), channel_id=1, source_target_pairs={{0,8},{8,16},{16,24},{1,9},{9,17},{17,25},{2,10},{10,18},{18,26},{... | collective-permute-start | bytes 1572872 | tf_op jit(solution)/shard_map/ppermute | solution.py:16
  14.3 10.6 %copy-start.28 = (bf16[1,1,128,2048]{3,2,1,0:T(8,128)(2,1)}, bf16[1,1,128,2048]{3,2,1,0:T(8,128)(2,1)S(1)}, u32[]{:S(2)}) copy-start(bf16[1,1,128,2048]{3,2,1,0:T(8,128)(2,1)S(1)} %collective-permute-done) | copy-start | bytes 1572868
  15.7 35.2 %collective-permute-start.3 = (bf16[3,1,128,2048]{3,2,1,0:T(8,128)(2,1)}, bf16[3,1,128,2048]{3,2,1,0:T(8,128)(2,1)}, u32[]{:S(2)}, u32[]{:S(2)}) collective-permute-start(bf16[3,1,128,2048]{3,2,1,0:T(8,128)(2,1)} %pad_maximum_fusion.1), channel_id=1, source_target_pairs={{1,0},{2,1},{3,2},{4,3},{5,4},{6,5},{7,6},{9,8},{10,9},{11,10},{12... | collective-permute-start | bytes 4718600 | tf_op jit(solution)/shard_map/ppermute | solution.py:19
  17.0 73.2 %collective-permute-start.2 = (bf16[3,1,128,2048]{3,2,1,0:T(8,128)(2,1)}, bf16[3,1,128,2048]{3,2,1,0:T(8,128)(2,1)}, u32[]{:S(2)}, u32[]{:S(2)}) collective-permute-start(bf16[3,1,128,2048]{3,2,1,0:T(8,128)(2,1)} %pad_maximum_fusion.1), channel_id=1, source_target_pairs={{0,1},{1,2},{2,3},{3,4},{4,5},{5,6},{6,7},{8,9},{9,10},{10,11},{11... | collective-permute-start | bytes 4718600 | tf_op jit(solution)/shard_map/ppermute | solution.py:16
  24.4 7.4 %copy-start.52 = (s32[1,9]{1,0:T(1,128)S(1)}, s32[1,9]{1,0:T(1,128)}, u32[]{:S(2)}) copy-start(s32[1,9]{1,0:T(1,128)} %param.12) | copy-start | bytes 112
  95.5 9.7 %copy-start.17 = (bf16[1152,256]{0,1:T(8,128)(2,1)}, bf16[1152,256]{0,1:T(8,128)(2,1)S(1)}, u32[]{:S(2)}) copy-start(bf16[1152,256]{0,1:T(8,128)(2,1)S(1)} %copy.131) | copy-start | bytes 1769476
  97.9 6.4 %copy-start.18 = (bf16[1152,256]{0,1:T(8,128)(2,1)}, bf16[1152,256]{0,1:T(8,128)(2,1)S(1)}, u32[]{:S(2)}) copy-start(bf16[1152,256]{0,1:T(8,128)(2,1)S(1)} %copy.129) | copy-start | bytes 1769476
  104.4 6.9 %copy-start.4 = (f32[4,128,1152]{1,2,0:T(8,128)}, f32[4,128,1152]{1,2,0:T(8,128)S(1)}, u32[]{:S(2)}) copy-start(f32[4,128,1152]{1,2,0:T(8,128)S(1)} %get-tuple-element.36) | copy-start | bytes 7077892
  105.1 10.0 %copy-start.2 = (f32[4,128,1152]{1,2,0:T(8,128)}, f32[4,128,1152]{1,2,0:T(8,128)S(1)}, u32[]{:S(2)}) copy-start(f32[4,128,1152]{1,2,0:T(8,128)S(1)} %get-tuple-element.38) | copy-start | bytes 7077892
  119.2 149.4 %all-gather.3.cloned.1.call-start = ((), (), s32[]{:S(2)}) async-start(), calls=%async_computation.2 | async-start | bytes 2621440 | tf_op jit(solution)/shard_map/all_gather | solution.py:128
  141.3 67.1 %collective-permute-start.5 = (f32[3,128,2048]{2,1,0:T(8,128)}, f32[3,128,2048]{2,1,0:T(8,128)}, u32[]{:S(2)}, u32[]{:S(2)}) collective-permute-start(f32[3,128,2048]{2,1,0:T(8,128)} %bitcast.170), channel_id=1, source_target_pairs={{0,8},{8,16},{16,24},{1,9},{9,17},{17,25},{2,10},{10,18},{18,26},{... | collective-permute-start | bytes 9437192 | tf_op jit(solution)/shard_map/ppermute | solution.py:27
  145.1 63.3 %collective-permute-start.4 = (f32[3,128,2048]{2,1,0:T(8,128)}, f32[3,128,2048]{2,1,0:T(8,128)}, u32[]{:S(2)}, u32[]{:S(2)}) collective-permute-start(f32[3,128,2048]{2,1,0:T(8,128)} %bitcast.169), channel_id=1, source_target_pairs={{8,0},{16,8},{24,16},{9,1},{17,9},{25,17},{10,2},{18,10},{26,18},{... | collective-permute-start | bytes 9437192 | tf_op jit(solution)/shard_map/ppermute | solution.py:27
  214.9 8.6 %copy-start.10 = (bf16[4,128,1152]{1,2,0:T(8,128)(2,1)S(1)}, bf16[4,128,1152]{1,2,0:T(8,128)(2,1)}, u32[]{:S(2)}) copy-start(bf16[4,128,1152]{1,2,0:T(8,128)(2,1)} %copy-done.9) | copy-start | bytes 3538948
  214.9 8.6 %copy-start.21 = (bf16[1152,256]{0,1:T(8,128)(2,1)S(1)}, bf16[1152,256]{0,1:T(8,128)(2,1)}, u32[]{:S(2)}) copy-start(bf16[1152,256]{0,1:T(8,128)(2,1)} %copy-done.20) | copy-start | bytes 1769476
  214.9 11.2 %copy-start.12 = (bf16[4,128,1152]{1,2,0:T(8,128)(2,1)S(1)}, bf16[4,128,1152]{1,2,0:T(8,128)(2,1)}, u32[]{:S(2)}) copy-start(bf16[4,128,1152]{1,2,0:T(8,128)(2,1)} %copy-done.11) | copy-start | bytes 3538948
  216.3 12.8 %copy-start.14 = (bf16[4,128,1152]{1,2,0:T(8,128)(2,1)S(1)}, bf16[4,128,1152]{1,2,0:T(8,128)(2,1)}, u32[]{:S(2)}) copy-start(bf16[4,128,1152]{1,2,0:T(8,128)(2,1)} %copy-done.13) | copy-start | bytes 3538948
  216.3 26.9 %collective-permute-start.6 = (f32[128,2048]{1,0:T(8,128)}, f32[128,2048]{1,0:T(8,128)}, u32[]{:S(2)}, u32[]{:S(2)}) collective-permute-start(f32[128,2048]{1,0:T(8,128)} %get-tuple-element.19), channel_id=1, source_target_pairs={{1,0},{2,1},{3,2},{4,3},{5,4},{6,5},{7,6},{9,8},{10,9},{11,10},{12... | collective-permute-start | bytes 3145736 | tf_op jit(solution)/shard_map/ppermute | solution.py:27
  217.9 47.7 %collective-permute-start.7 = (f32[128,2048]{1,0:T(8,128)}, f32[128,2048]{1,0:T(8,128)}, u32[]{:S(2)}, u32[]{:S(2)}) collective-permute-start(f32[128,2048]{1,0:T(8,128)} %get-tuple-element.20), channel_id=1, source_target_pairs={{0,1},{1,2},{2,3},{3,4},{4,5},{5,6},{6,7},{8,9},{9,10},{10,11},{11... | collective-permute-start | bytes 3145736 | tf_op jit(solution)/shard_map/ppermute | solution.py:27
  224.4 6.3 %copy-start.16 = (bf16[4,128,1152]{1,2,0:T(8,128)(2,1)S(1)}, bf16[4,128,1152]{1,2,0:T(8,128)(2,1)}, u32[]{:S(2)}) copy-start(bf16[4,128,1152]{1,2,0:T(8,128)(2,1)} %copy-done.15) | copy-start | bytes 3538948
  265.6 5.7 %copy-start.1 = (bf16[1024,1024]{1,0:T(8,128)(2,1)S(1)}, bf16[1024,1024]{1,0:T(8,128)(2,1)}, u32[]{:S(2)}) copy-start(bf16[1024,1024]{1,0:T(8,128)(2,1)} %param.11) | copy-start | bytes 6291460
  (39 other events, 80.9 us)
Sparse Core Ops, SparseCore 0:
  119.3 89.0 reduce-scatter.1
  209.9 22.1 all-gather.2
